TPU v7x, 256 devices: a whole 4x4x8 slice. The times are simulated.
256 devices in a mesh: rep: 64 (over z, x, core), tp: 4 (over y).
Axes of the slice: x: 4, y: 4, z: 8, core: 2. Of those that a mesh axis runs over, the one named last changes fastest.
Arguments:
- suffix_source: bfloat16 [64, 384, 4096], P('rep', None, 'tp'), may hold values from -6 to 6
- suffix_accept: bfloat16 [64, 384, 4096], P('rep', None, 'tp'), may hold values from -3 to 3
- suffix_address: bfloat16 [64, 384, 4096], P('rep', None, 'tp'), may hold values from -3 to 3
- guess_lane_source: bfloat16 [128, 16, 4096], P('rep', None, 'tp'), may hold values from -6 to 6
- guess_lane_accept: bfloat16 [128, 16, 4096], P('rep', None, 'tp'), may hold values from -3 to 3
- guess_lane_address: bfloat16 [128, 16, 4096], P('rep', None, 'tp'), may hold values from -3 to 3
- content_map: bfloat16 [4096, 4096], P(None, 'tp'), may hold values from -0.09375 to 0.09375
- forget_shrink_map: bfloat16 [4096, 128], replicated, may hold values from -0.09375 to 0.09375
- forget_expand_map: bfloat16 [128, 4096], P(None, 'tp'), may hold values from -0.35351562 to 0.35351562
- forget_lane_anchor: float32 [4096], P('tp'), may hold values from -12 to -3
- present_boost: float32 [4096], P('tp'), may hold values from -1.5 to 1.5
- content_blend_share: float32 [4096], P('tp'), may hold values from 0 to 1
- forget_blend_share: float32 [4096], P('tp'), may hold values from 0 to 1
- lane_normal_scale: float32 [4096], P('tp'), may hold values from 0.5 to 1.5
- lane_normal_shift: float32 [4096], P('tp'), may hold values from -1.2 to 1.2
- kernel_memory_saved: float32 [128, 64, 4096], P(None, 'rep', 'tp'), may hold values from -6 to 6
- prior_source_saved: bfloat16 [128, 64, 64], P(None, 'rep', 'tp'), may hold values from -6 to 6
- lane_owner: int32 [128], replicated, may hold values from 0 to 127, as said below
- request_spans: int32 [128], replicated, may hold values from 16 to 400, as said below
- admitted_guesses: int32 [128], replicated, may hold values from 0 to 16
Outputs:
- tail_out: bfloat16 [64, 384, 4096], P('rep', None, 'tp')
- draft_out: bfloat16 [128, 16, 4096], P('rep', None, 'tp')
- state_out: float32 [128, 64, 4096], P(None, 'rep', 'tp')
- shift_out: bfloat16 [128, 64, 64], P(None, 'rep', 'tp')
Inputs may be any that keep to these rules, and one draw needn't show every extreme that they name: `lane_owner`: a permutation of the request numbers. `request_spans`: exactly 8 requests have 16 + 384 tokens and the others 16; a long request is always dealt to a slot s with s % 2 == 0; each aligned block of 8 consecutive groups holds exactly one group whose first slot is long; the tail buffers of groups whose first slot is not long are not read.
All inputs are finite; a program needn't handle non-finite values.
Results may differ from a plain program's by a relative error of at most 0.0051.
The roundings to bfloat16 on the way count: a program that leaves them out, or rounds other values in their place, can miss the bound.
Values may be sent and summed in bfloat16 or wider, within the bound.
A program may use at most 128 MiB of HBM per device.

v0:
```python
import jax
import jax.numpy as jnp
from jax import lax
from jax.sharding import PartitionSpec as P

SUBSPACE_SPAN = 64
DRAFT = 16
HIGH = lax.Precision.HIGHEST
EPS = 0.00064


def group_norm(answer_collection, lane_normal_scale, lane_normal_shift):
    center = answer_collection - jnp.mean(answer_collection, axis=-1, keepdims=True)
    spread = jnp.mean(center * center, axis=-1, keepdims=True)
    normed = (center / jnp.sqrt(spread + EPS)).reshape(answer_collection.shape[0], -1)
    return (normed * lane_normal_scale + lane_normal_shift).astype(jnp.bfloat16)


def token_mix(current, previous, mixing):
    present = current.astype(jnp.float32)
    return (present + (previous.astype(jnp.float32) - present) * mixing).astype(jnp.bfloat16)


def project(
    mixed_value,
    decay_mixed_input,
    content_map,
    forget_shrink_map,
    forget_expand_map,
    forget_lane_anchor,
):
    acc_value = jnp.dot(
        lax.all_gather(mixed_value, "tp", axis=1, tiled=True),
        content_map,
        preferred_element_type=jnp.float32,
    )
    decay_accumulated = jnp.dot(
        lax.all_gather(decay_mixed_input, "tp", axis=1, tiled=True),
        forget_shrink_map,
        preferred_element_type=jnp.float32,
    )
    acc_value, decay_accumulated = (acc_value, decay_accumulated)
    content_vectors = acc_value.astype(jnp.bfloat16)
    decay_low_rank = jnp.tanh(decay_accumulated).astype(jnp.bfloat16)
    forget_logscale = -jnp.exp(
        forget_lane_anchor
        + jnp.dot(decay_low_rank, forget_expand_map, preferred_element_type=jnp.float32)
    )
    return (content_vectors, forget_logscale)


def process_blocks(
    accept_vectors, address_vectors, content_vectors, forget_logscale, ongoing_memory, lanes_boost
):
    total_steps = accept_vectors.shape[0]
    block_len = min(64, total_steps)
    block_count = total_steps // block_len
    lower = jnp.arange(block_len)[:, None] > jnp.arange(block_len)[None, :]

    def shape_blocks(array):
        return array.reshape(block_count, block_len, array.shape[1], array.shape[2])

    def one_block(threaded_pair, source_vectors):
        accept_vectors_all, address_vectors_all, value_rows_batch, rate_b = source_vectors
        inclusive = jnp.cumsum(rate_b, axis=0)
        exclusive = inclusive - rate_b
        middle = inclusive[block_len // 2]
        recept_scaled = accept_vectors_all * jnp.exp(exclusive - middle)
        keys_scaled = address_vectors_all * jnp.exp(middle - inclusive)
        scores = jnp.einsum("thi,shi->hts", recept_scaled, keys_scaled, precision=HIGH)
        scores = jnp.where(lower[None], scores, 0.0)
        answer_vectors = jnp.einsum("hts,shj->thj", scores, value_rows_batch, precision=HIGH)
        answer_vectors = answer_vectors + jnp.einsum(
            "thi,hij->thj", accept_vectors_all * jnp.exp(exclusive), threaded_pair, precision=HIGH
        )
        answer_vectors = (
            answer_vectors
            + jnp.sum(
                accept_vectors_all * lanes_boost * address_vectors_all, axis=-1, keepdims=True
            )
            * value_rows_batch
        )
        total = inclusive[-1]
        threaded_pair = jnp.exp(total)[:, :, None] * threaded_pair + jnp.einsum(
            "shi,shj->hij",
            address_vectors_all * jnp.exp(total - inclusive),
            value_rows_batch,
            precision=HIGH,
        )
        return (threaded_pair, answer_vectors)

    closing_answer, answer_collection = lax.scan(
        one_block,
        ongoing_memory,
        (
            shape_blocks(accept_vectors),
            shape_blocks(address_vectors),
            shape_blocks(content_vectors),
            shape_blocks(forget_logscale),
        ),
    )
    return (
        answer_collection.reshape(total_steps, accept_vectors.shape[1], accept_vectors.shape[2]),
        closing_answer,
    )


def local(
    suffix_source,
    suffix_accept,
    suffix_address,
    guess_lane_source,
    guess_lane_accept,
    guess_lane_address,
    content_map,
    forget_shrink_map,
    forget_expand_map,
    forget_lane_anchor,
    present_boost,
    content_blend_share,
    forget_blend_share,
    lane_normal_scale,
    lane_normal_shift,
    kernel_memory_saved,
    prior_source_saved,
    lane_owner,
    request_spans,
    admitted_guesses,
):
    local_width = content_map.shape[1]
    lanes_owned = local_width // SUBSPACE_SPAN
    slots = guess_lane_source.shape[0]
    squad_index = lax.axis_index("rep")
    slot_ids = squad_index * slots + jnp.arange(slots, dtype=jnp.int32)
    my_reqs = lane_owner[slot_ids]
    slot_long = request_spans[my_reqs] > DRAFT
    group_long = slot_long[0]
    lanes_boost = present_boost.reshape(lanes_owned, SUBSPACE_SPAN)
    ordered_state = kernel_memory_saved[lane_owner]
    ordered_shift = prior_source_saved[lane_owner].astype(jnp.float32)
    got_state, got_shift = (
        lax.all_to_all(ordered_state, "rep", split_axis=0, concat_axis=1, tiled=True),
        lax.all_to_all(ordered_shift, "rep", split_axis=0, concat_axis=1, tiled=True),
    )
    start = got_state.reshape(slots, SUBSPACE_SPAN, lanes_owned, SUBSPACE_SPAN).transpose(
        0, 2, 1, 3
    )
    start_prev = got_shift.astype(jnp.bfloat16).transpose(0, 2, 1).reshape(slots, local_width)

    def divide_lanes(array):
        return array.astype(jnp.float32).reshape(array.shape[0], lanes_owned, SUBSPACE_SPAN)

    tail_tokens = suffix_source[0]
    tail_len = tail_tokens.shape[0]
    tail_prev = jnp.concatenate([start_prev[:1], tail_tokens[:-1]], axis=0)
    tail_value = token_mix(tail_tokens, tail_prev, content_blend_share)
    tail_decay = token_mix(tail_tokens, tail_prev, forget_blend_share)
    tail_recept = suffix_accept[0]
    tail_keys = suffix_address[0]
    first = jnp.where(slot_long[:, None], tail_tokens[-1][None, :], start_prev)
    draft_prev = jnp.concatenate([first[:, None], guess_lane_source[:, :-1]], axis=1)
    draft_value = token_mix(guess_lane_source, draft_prev, content_blend_share).reshape(
        slots * DRAFT, local_width
    )
    draft_decay = token_mix(guess_lane_source, draft_prev, forget_blend_share).reshape(
        slots * DRAFT, local_width
    )
    content_vectors, forget_logscale = project(
        jnp.concatenate([tail_value, draft_value], axis=0),
        jnp.concatenate([tail_decay, draft_decay], axis=0),
        content_map,
        forget_shrink_map,
        forget_expand_map,
        forget_lane_anchor,
    )
    tail_y, tail_end = process_blocks(
        divide_lanes(tail_recept),
        divide_lanes(tail_keys),
        divide_lanes(content_vectors[:tail_len]),
        forget_logscale[:tail_len].reshape(tail_len, lanes_owned, SUBSPACE_SPAN),
        start[0],
        lanes_boost,
    )
    tail_norm = group_norm(tail_y, lane_normal_scale, lane_normal_shift)
    tail_out = jnp.where(group_long, tail_norm, jnp.zeros_like(tail_norm))[None]
    guess_content = (
        content_vectors[tail_len:]
        .astype(jnp.float32)
        .reshape(slots, DRAFT, lanes_owned, SUBSPACE_SPAN)
    )
    guess_forget = forget_logscale[tail_len:].reshape(slots, DRAFT, lanes_owned, SUBSPACE_SPAN)
    guess_accept = guess_lane_accept.astype(jnp.float32).reshape(
        slots, DRAFT, lanes_owned, SUBSPACE_SPAN
    )
    guess_address = guess_lane_address.astype(jnp.float32).reshape(
        slots, DRAFT, lanes_owned, SUBSPACE_SPAN
    )
    trailing_pair = jnp.where(slot_long[:, None, None, None], tail_end[None], start)
    draft_y, draft_final = jax.vmap(process_blocks, in_axes=(0, 0, 0, 0, 0, None))(
        guess_accept, guess_address, guess_content, guess_forget, trailing_pair, lanes_boost
    )
    draft_out = group_norm(
        draft_y.reshape(slots * DRAFT, lanes_owned, SUBSPACE_SPAN),
        lane_normal_scale,
        lane_normal_shift,
    ).reshape(slots, DRAFT, local_width)
    count = admitted_guesses[my_reqs]
    taken = jnp.arange(DRAFT, dtype=jnp.int32)[None, :] < count[:, None]
    inclusive_d = jnp.cumsum(guess_forget, axis=1)
    upto = jnp.sum(jnp.where(taken[:, :, None, None], guess_forget, 0.0), axis=1)
    weight = jnp.where(taken[:, :, None, None], jnp.exp(upto[:, None] - inclusive_d), 0.0)
    chosen = jnp.exp(upto)[..., None] * trailing_pair + jnp.einsum(
        "sthi,sthj->shij", guess_address * weight, guess_content, precision=HIGH
    )
    edge_row = guess_lane_source[jnp.arange(slots), jnp.maximum(count - 1, 0)]
    edge = jnp.where((count > 0)[:, None], edge_row, first)
    ret_state = chosen.transpose(0, 2, 1, 3).reshape(slots, SUBSPACE_SPAN, local_width)
    ret_shift = (
        edge.reshape(slots, lanes_owned, SUBSPACE_SPAN).transpose(0, 2, 1).astype(jnp.float32)
    )
    back_state, back_shift = (
        lax.all_to_all(ret_state, "rep", split_axis=1, concat_axis=0, tiled=True),
        lax.all_to_all(ret_shift, "rep", split_axis=1, concat_axis=0, tiled=True),
    )
    total_reqs = lane_owner.shape[0]
    inverse = (
        jnp.zeros((total_reqs,), jnp.int32)
        .at[lane_owner]
        .set(jnp.arange(total_reqs, dtype=jnp.int32))
    )
    state_out = back_state[inverse]
    shift_out = back_shift[inverse].astype(jnp.bfloat16)
    return (tail_out, draft_out, state_out, shift_out)


def solution(mesh):
    placed = (
        P("rep", None, "tp"),
        P("rep", None, "tp"),
        P("rep", None, "tp"),
        P("rep", None, "tp"),
        P("rep", None, "tp"),
        P("rep", None, "tp"),
        P(None, "tp"),
        P(),
        P(None, "tp"),
        P("tp"),
        P("tp"),
        P("tp"),
        P("tp"),
        P("tp"),
        P("tp"),
        P(None, "rep", "tp"),
        P(None, "rep", "tp"),
        P(),
        P(),
        P(),
    )
    return jax.shard_map(
        local,
        mesh=mesh,
        in_specs=placed,
        out_specs=(
            P("rep", None, "tp"),
            P("rep", None, "tp"),
            P(None, "rep", "tp"),
            P(None, "rep", "tp"),
        ),
        check_vma=False,
    )
```

profile of v0, /device:TPU:1, one launch (start us, length us, event | category | flops | bytes accessed | tf_op | source)
XLA Modules:
  0.0 245.0 jit_solution(6929239159110475393)
XLA Ops:
  10.2 13.0 %all-to-all-start.1 = ((bf16[128,1,16]{2,1,0:T(2,128)(2,1)}), bf16[128,1,16]{2,1,0:T(2,128)(2,1)S(1)}, u32[]{:S(2)}, u32[]{:S(2)}) async-start(bf16[128,1,16]{2,1,0:T(2,128)(2,1)} %convert.36), calls=%async_computation.1 | async-start | bytes 131072 | tf_op jit(solution)/shard_map/all_to_all | solution.py:143
  26.0 7.3 %all-to-all-done.1 = bf16[128,1,16]{2,1,0:T(2,128)(2,1)S(1)} async-done(((bf16[128,1,16]{2,1,0:T(2,128)(2,1)}), bf16[128,1,16]{2,1,0:T(2,128)(2,1)S(1)}, u32[]{:S(2)}, u32[]{:S(2)}) %all-to-all-start.1) | async-done | bytes 4128 | tf_op jit(solution)/shard_map/all_to_all | solution.py:143
  39.5 4.4 %all-to-all-start.3 = ((bf16[2,64,16]{2,0,1:T(2,128)(2,1)}), bf16[2,64,16]{2,0,1:T(2,128)(2,1)S(1)}, u32[]{:S(2)}, u32[]{:S(2)}) async-start(bf16[2,64,16]{2,0,1:T(2,128)(2,1)} %convert_bitcast_fusion), calls=%async_computation.3 | async-start | bytes 65536 | tf_op jit(solution)/shard_map/all_to_all | solution.py:223
  46.2 7.1 %all-to-all-done.3 = bf16[2,64,16]{2,0,1:T(2,128)(2,1)S(1)} async-done(((bf16[2,64,16]{2,0,1:T(2,128)(2,1)}), bf16[2,64,16]{2,0,1:T(2,128)(2,1)S(1)}, u32[]{:S(2)}, u32[]{:S(2)}) %all-to-all-start.3) | async-done | bytes 4128 | tf_op jit(solution)/shard_map/all_to_all | solution.py:223
  53.3 4.7 %all-to-all-start = ((f32[128,1,1024]{2,1,0:T(1,128)}), f32[128,1,1024]{2,1,0:T(1,128)S(1)}, u32[]{:S(2)}, u32[]{:S(2)}) async-start(f32[128,1,1024]{2,1,0:T(1,128)} %copy.156), calls=%async_computation | async-start | bytes 1048576 | tf_op jit(solution)/shard_map/all_to_all | solution.py:142
  61.0 2.2 reshape.402
  63.2 3.4 %reshape.400 = f32[6,64,16,64]{3,2,1,0:T(8,128)} reshape(bf16[1,384,1024]{2,1,0:T(8,128)(2,1)} %param.24) | data formatting | bytes 2359296 | tf_op jit(solution)/shard_map/convert_element_type | solution.py:151
  69.2 6.7 %all-to-all-done = f32[128,1,1024]{2,1,0:T(1,128)S(1)} async-done(((f32[128,1,1024]{2,1,0:T(1,128)}), f32[128,1,1024]{2,1,0:T(1,128)S(1)}, u32[]{:S(2)}, u32[]{:S(2)}) %all-to-all-start) | async-done | bytes 524320 | tf_op jit(solution)/shard_map/all_to_all | solution.py:142
  77.6 8.1 %convolution_convert_fusion = bf16[416,1024]{1,0:T(8,128)(2,1)S(1)} fusion(bf16[416,4096]{1,0:T(8,128)(2,1)} %all-gather.5.cloned.1.call-done, bf16[4096,1024]{1,0:T(8,128)(2,1)} %param.28), kind=kOutput, calls=%fused_computation.48 | convolution fusion | flops 3490086912 | bytes 12648448 | tf_op jit(solution)/shard_map/dot_general | solution.py:32
  87.7 33.6 %all-gather.3.cloned.1.call-done = bf16[416,4096]{1,0:T(8,128)(2,1)} async-done(((bf16[416,1024]{1,0:T(8,128)(2,1)}), bf16[416,4096]{1,0:T(8,128)(2,1)}) %all-gather.3.cloned.1.call-update) | async-done | bytes 3407888 | tf_op jit(solution)/shard_map/all_gather | solution.py:38
  121.3 3.7 %exponential_negate_fusion = f32[416,1024]{1,0:T(8,128)S(1)} fusion(bf16[128,1024]{1,0:T(8,128)(2,1)S(1)} %copy-done.18, bf16[416,4096]{1,0:T(8,128)(2,1)} %all-gather.3.cloned.1.call-done, bf16[4096,128]{1,0:T(8,128)(2,1)S(1)} %copy-done, f32[1024]{0:T(1024)} %param.31), kind=kOutput, calls=%fused_computation.44 | convolution fusion | flops 546164736 | bytes 6426624 | tf_op jit(solution)/shard_map/dot_general | solution.py:47
  129.2 2.2 reshape_reshape.7
  131.4 3.4 %reshape.401 = f32[6,64,16,64]{3,2,1,0:T(8,128)} reshape(f32[384,1024]{1,0:T(8,128)} %slice_convert_fusion) | data formatting | bytes 3145728 | tf_op jit(solution)/shard_map/reshape;reshape | solution.py:61
  134.8 60.3 %while.3 = (s32[]{:T(128)}, f32[16,64,64]{2,1,0:T(8,128)S(1)}, f32[6,64,16,64]{3,1,2,0:T(8,128)}, f32[6,64,16,64]{3,2,1,0:T(8,128)}, f32[6,64,16,64]{3,2,1,0:T(8...) while((s32[]{:T(128)}, f32[16,64,64]{2,1,0:T(8,128)S(1)}, ...), condition=%wide.region_3.4_spmd.clone, body=%wide.region_0.3_spmd.clone.sunk | while | flops 206572544 | bytes 8724625 | solution.py:92
  137.1 2.5 %bitcast_multiply_fusion.6 = (f32[64,16,64]{2,1,0:T(8,128)S(1)}, f32[64,16,64]{2,1,0:T(8,128)S(1)}, f32[64,16]{1,0:T(8,128)S(1)}, f32[64,16,64]{2,1,0:T(8,128)S(1)}, f32[64,16,64]{2,1,0:T(8,128)}) fusion(f32[64,16,64]{2,1,0:T(8,128)S(1)} %fusion.68, f32[6,64,16,64]{3,2,1,0:T(8,128)} %get-tuple-element.282, s32[]{:T(128)S(6)} %copy.261, ...), kind=kLoop, calls=%fused_computation.24.clone.1 | loop fusion | flops 719872 | bytes 2113540 | tf_op jit(solution)/shard_map/while/body/eval_jaxpr/mul | solution.py:69
  141.7 1.8 fusion.70
  147.1 2.5 %bitcast_multiply_fusion.6 = (f32[64,16,64]{2,1,0:T(8,128)S(1)}, f32[64,16,64]{2,1,0:T(8,128)S(1)}, f32[64,16]{1,0:T(8,128)S(1)}, f32[64,16,64]{2,1,0:T(8,128)S(1)}, f32[64,16,64]{2,1,0:T(8,128)}) fusion(f32[64,16,64]{2,1,0:T(8,128)S(1)} %fusion.68, f32[6,64,16,64]{3,2,1,0:T(8,128)} %get-tuple-element.282, s32[]{:T(128)S(6)} %copy.261, ...), kind=kLoop, calls=%fused_computation.24.clone.1 | loop fusion | flops 719872 | bytes 2113540 | tf_op jit(solution)/shard_map/while/body/eval_jaxpr/mul | solution.py:69
  151.8 1.8 fusion.70
  157.2 2.5 %bitcast_multiply_fusion.6 = (f32[64,16,64]{2,1,0:T(8,128)S(1)}, f32[64,16,64]{2,1,0:T(8,128)S(1)}, f32[64,16]{1,0:T(8,128)S(1)}, f32[64,16,64]{2,1,0:T(8,128)S(1)}, f32[64,16,64]{2,1,0:T(8,128)}) fusion(f32[64,16,64]{2,1,0:T(8,128)S(1)} %fusion.68, f32[6,64,16,64]{3,2,1,0:T(8,128)} %get-tuple-element.282, s32[]{:T(128)S(6)} %copy.261, ...), kind=kLoop, calls=%fused_computation.24.clone.1 | loop fusion | flops 719872 | bytes 2113540 | tf_op jit(solution)/shard_map/while/body/eval_jaxpr/mul | solution.py:69
  161.8 1.8 fusion.70
  167.2 2.5 %bitcast_multiply_fusion.6 = (f32[64,16,64]{2,1,0:T(8,128)S(1)}, f32[64,16,64]{2,1,0:T(8,128)S(1)}, f32[64,16]{1,0:T(8,128)S(1)}, f32[64,16,64]{2,1,0:T(8,128)S(1)}, f32[64,16,64]{2,1,0:T(8,128)}) fusion(f32[64,16,64]{2,1,0:T(8,128)S(1)} %fusion.68, f32[6,64,16,64]{3,2,1,0:T(8,128)} %get-tuple-element.282, s32[]{:T(128)S(6)} %copy.261, ...), kind=kLoop, calls=%fused_computation.24.clone.1 | loop fusion | flops 719872 | bytes 2113540 | tf_op jit(solution)/shard_map/while/body/eval_jaxpr/mul | solution.py:69
  171.9 1.8 fusion.70
  177.3 2.5 %bitcast_multiply_fusion.6 = (f32[64,16,64]{2,1,0:T(8,128)S(1)}, f32[64,16,64]{2,1,0:T(8,128)S(1)}, f32[64,16]{1,0:T(8,128)S(1)}, f32[64,16,64]{2,1,0:T(8,128)S(1)}, f32[64,16,64]{2,1,0:T(8,128)}) fusion(f32[64,16,64]{2,1,0:T(8,128)S(1)} %fusion.68, f32[6,64,16,64]{3,2,1,0:T(8,128)} %get-tuple-element.282, s32[]{:T(128)S(6)} %copy.261, ...), kind=kLoop, calls=%fused_computation.24.clone.1 | loop fusion | flops 719872 | bytes 2113540 | tf_op jit(solution)/shard_map/while/body/eval_jaxpr/mul | solution.py:69
  182.0 1.8 fusion.70
  187.3 2.5 %bitcast_multiply_fusion.6 = (f32[64,16,64]{2,1,0:T(8,128)S(1)}, f32[64,16,64]{2,1,0:T(8,128)S(1)}, f32[64,16]{1,0:T(8,128)S(1)}, f32[64,16,64]{2,1,0:T(8,128)S(1)}, f32[64,16,64]{2,1,0:T(8,128)}) fusion(f32[64,16,64]{2,1,0:T(8,128)S(1)} %fusion.68, f32[6,64,16,64]{3,2,1,0:T(8,128)} %get-tuple-element.282, s32[]{:T(128)S(6)} %copy.261, ...), kind=kLoop, calls=%fused_computation.24.clone.1 | loop fusion | flops 719872 | bytes 2113540 | tf_op jit(solution)/shard_map/while/body/eval_jaxpr/mul | solution.py:69
  192.0 1.8 fusion.70
  195.1 2.8 %reduce_sum.64 = f32[6,64,16]{1,2,0:T(8,128)S(1)} reduce(f32[6,64,16,64]{3,1,2,0:T(8,128)} %get-tuple-element.79, f32[]{:T(128)} %constant.69.clone.1), dimensions={3}, to_apply=%region_4.5 | reduce | flops 387072 | bytes 1597444 | tf_op jit(solution)/shard_map/reduce_sum | solution.py:13
  197.9 3.3 %multiply_reduce_fusion = f32[6,64,16]{1,2,0:T(8,128)S(1)} fusion(f32[6,64,16,64]{3,1,2,0:T(8,128)} %get-tuple-element.79, f32[6,64,16]{1,2,0:T(8,128)S(1)} %broadcast_multiply_fusion), kind=kLoop, calls=%fused_computation.40 | loop fusion | flops 1173504 | bytes 1622016 | tf_op jit(solution)/shard_map/reduce_sum | solution.py:14
  205.5 10.8 %all-to-all-start.2 = ((f32[2,64,1024]{2,0,1:T(2,128)}), f32[2,64,1024]{2,0,1:T(2,128)S(1)}, u32[]{:S(2)}, u32[]{:S(2)}) async-start(f32[2,64,1024]{2,0,1:T(2,128)} %reshape.497), calls=%async_computation.2 | async-start | bytes 1048576 | tf_op jit(solution)/shard_map/all_to_all | solution.py:222
  218.9 3.5 %copy.165 = f32[6,64,16,64]{3,2,1,0:T(8,128)} copy(f32[6,64,16,64]{3,1,2,0:T(8,128)S(1)} %copy-done.4) | data formatting | bytes 3145728 | tf_op jit(solution)/shard_map/while | solution.py:92
  222.3 3.7 %reshape.397 = f32[1,384,1024]{2,1,0:T(8,128)} reshape(f32[6,64,16,64]{3,2,1,0:T(8,128)} %copy.165) | data formatting | bytes 3145728 | tf_op jit(solution)/shard_map/reshape | solution.py:103
  231.5 3.9 %fusion.26 = bf16[1,384,1024]{2,1,0:T(8,128)(2,1)} fusion(f32[1024]{0:T(1024)S(1)} %copy-done.26, f32[1024]{0:T(1024)S(1)} %copy-done.27, f32[1,384,1024]{2,1,0:T(8,128)} %copy.169, f32[1,384,1024]{2,1,0:T(8,128)} %reshape.397, f32[1,384,1024]{2,1,0:T(8,128)} %copy.167, pred[]{:T(512)S(1)} %bitcast.201), kind=kLoop, calls=%fused_computation.66 | loop fusion | flops 2359296 | bytes 5513217 | tf_op jit(solution)/shard_map/jit(_where)/select_n | solution.py:185
  (238 shorter events, 76.5 us)
Async XLA Ops:
  7.2 114.1 %copy-start = (bf16[4096,128]{1,0:T(8,128)(2,1)S(1)}, bf16[4096,128]{1,0:T(8,128)(2,1)}, u32[]{:S(2)}) copy-start(bf16[4096,128]{1,0:T(8,128)(2,1)} %param.29) | copy-start | bytes 3145732
  7.2 18.7 %copy-start.8 = (bf16[1,384,1024]{2,1,0:T(8,128)(2,1)S(1)}, bf16[1,384,1024]{2,1,0:T(8,128)(2,1)}, u32[]{:S(2)}) copy-start(bf16[1,384,1024]{2,1,0:T(8,128)(2,1)} %param.22) | copy-start | bytes 2359300
  8.8 25.0 %copy-start.17 = (bf16[2,16,1024]{2,1,0:T(8,128)(2,1)S(1)}, bf16[2,16,1024]{2,1,0:T(8,128)(2,1)}, u32[]{:S(2)}) copy-start(bf16[2,16,1024]{2,1,0:T(8,128)(2,1)} %param.25) | copy-start | bytes 196612
  8.8 25.0 %copy-start.24 = (f32[1024]{0:T(1024)S(1)}, f32[1024]{0:T(1024)}, u32[]{:S(2)}) copy-start(f32[1024]{0:T(1024)} %param.33) | copy-start | bytes 12292
  8.8 25.0 %copy-start.25 = (f32[1024]{0:T(1024)S(1)}, f32[1024]{0:T(1024)}, u32[]{:S(2)}) copy-start(f32[1024]{0:T(1024)} %param.34) | copy-start | bytes 12292
  10.2 23.1 %all-to-all-start.1 = ((bf16[128,1,16]{2,1,0:T(2,128)(2,1)}), bf16[128,1,16]{2,1,0:T(2,128)(2,1)S(1)}, u32[]{:S(2)}, u32[]{:S(2)}) async-start(bf16[128,1,16]{2,1,0:T(2,128)(2,1)} %convert.36), calls=%async_computation.1 | async-start | bytes 131072 | tf_op jit(solution)/shard_map/all_to_all | solution.py:143
  23.2 54.4 %all-gather.5.cloned.1.call-start = ((), (), s32[]{:S(2)}) async-start(), calls=%async_computation.5 | async-start | bytes 4259840 | tf_op jit(solution)/shard_map/all_gather | solution.py:33
  36.0 7.9 %copy-start.16 = (f32[128,1,1024]{2,1,0:T(1,128)S(1)}, f32[128,1,1024]{2,1,0:T(1,128)}, u32[]{:S(2)}) copy-start(f32[128,1,1024]{2,1,0:T(1,128)} %param.37) | copy-start | bytes 1572868
  36.0 85.2 %all-gather.3.cloned.1.call-start = ((), (), s32[]{:S(2)}) async-start(), calls=%async_computation.4 | async-start | bytes 4259840 | tf_op jit(solution)/shard_map/all_gather | solution.py:38
  39.5 13.8 %all-to-all-start.3 = ((bf16[2,64,16]{2,0,1:T(2,128)(2,1)}), bf16[2,64,16]{2,0,1:T(2,128)(2,1)S(1)}, u32[]{:S(2)}, u32[]{:S(2)}) async-start(bf16[2,64,16]{2,0,1:T(2,128)(2,1)} %convert_bitcast_fusion), calls=%async_computation.3 | async-start | bytes 65536 | tf_op jit(solution)/shard_map/all_to_all | solution.py:223
  44.8 14.4 %copy-start.21 = (f32[1024]{0:T(1024)S(1)}, f32[1024]{0:T(1024)}, u32[]{:S(2)}) copy-start(f32[1024]{0:T(1024)} %param.32) | copy-start | bytes 12292
  44.8 14.5 %copy-start.22 = (bf16[2,16,1024]{2,1,0:T(8,128)(2,1)S(1)}, bf16[2,16,1024]{2,1,0:T(8,128)(2,1)}, u32[]{:S(2)}) copy-start(bf16[2,16,1024]{2,1,0:T(8,128)(2,1)} %param.26) | copy-start | bytes 196612
  44.8 15.3 %copy-start.23 = (bf16[2,16,1024]{2,1,0:T(8,128)(2,1)S(1)}, bf16[2,16,1024]{2,1,0:T(8,128)(2,1)}, u32[]{:S(2)}) copy-start(bf16[2,16,1024]{2,1,0:T(8,128)(2,1)} %param.27) | copy-start | bytes 196612
  44.9 16.2 %copy-start.15 = (bf16[1,384,1024]{2,1,0:T(8,128)(2,1)S(1)}, bf16[1,384,1024]{2,1,0:T(8,128)(2,1)}, u32[]{:S(2)}) copy-start(bf16[1,384,1024]{2,1,0:T(8,128)(2,1)} %param.23) | copy-start | bytes 2359300
  53.3 22.6 %all-to-all-start = ((f32[128,1,1024]{2,1,0:T(1,128)}), f32[128,1,1024]{2,1,0:T(1,128)S(1)}, u32[]{:S(2)}, u32[]{:S(2)}) async-start(f32[128,1,1024]{2,1,0:T(1,128)} %copy.156), calls=%async_computation | async-start | bytes 1048576 | tf_op jit(solution)/shard_map/all_to_all | solution.py:142
  67.2 8.9 %copy-start.29 = (s32[1024]{0:T(1024)}, s32[1024]{0:T(1024)S(1)}, u32[]{:S(2)}) copy-start(s32[1024]{0:T(1024)S(1)} %pad_clamp_fusion) | copy-start | bytes 12292
  85.7 35.6 %copy-start.18 = (bf16[128,1024]{1,0:T(8,128)(2,1)S(1)}, bf16[128,1024]{1,0:T(8,128)(2,1)}, u32[]{:S(2)}) copy-start(bf16[128,1024]{1,0:T(8,128)(2,1)} %param.30) | copy-start | bytes 786436
  125.0 2.8 %copy-start.30 = (pred[2,16]{1,0:T(4,128)(4,1)S(1)}, pred[2,16]{1,0:T(4,128)(4,1)}, u32[]{:S(2)}) copy-start(pred[2,16]{1,0:T(4,128)(4,1)} %iota_compare_fusion.2) | copy-start | bytes 100
  125.0 2.9 %copy-start.12 = (f32[2,16,16,64]{3,2,1,0:T(8,128)S(1)}, f32[2,16,16,64]{3,2,1,0:T(8,128)}, u32[]{:S(2)}) copy-start(f32[2,16,16,64]{3,2,1,0:T(8,128)} %reshape.403) | copy-start | bytes 393220
  125.0 2.9 %copy-start.13 = (f32[2,16,16,64]{3,2,1,0:T(8,128)S(1)}, f32[2,16,16,64]{3,2,1,0:T(8,128)}, u32[]{:S(2)}) copy-start(f32[2,16,16,64]{3,2,1,0:T(8,128)} %reshape.404) | copy-start | bytes 393220
  126.3 2.9 %slice-start = ((f32[416,1024]{1,0:T(8,128)}), f32[384,1024]{1,0:T(8,128)S(1)}, s32[]{:S(2)}) async-start(f32[416,1024]{1,0:T(8,128)} %copy-done.7), calls=%async_computation.6 | async-start | bytes 3145728 | tf_op jit(solution)/shard_map/slice | solution.py:180
  139.7 2.1 copy-start.3
  159.8 2.1 copy-start.3
  179.9 2.1 copy-start.3
  197.9 3.7 %copy-start.6 = (f32[2,64,16,64]{3,2,1,0:T(8,128)S(1)}, f32[2,64,16,64]{3,2,1,0:T(8,128)}, u32[]{:S(2)}) copy-start(f32[2,64,16,64]{3,2,1,0:T(8,128)} %copy-done.5) | copy-start | bytes 1572868
  204.2 12.2 %copy-start.14 = (f32[2,16,16,64]{3,2,1,0:T(8,128)S(1)}, f32[2,16,16,64]{3,2,1,0:T(8,128)}, u32[]{:S(2)}) copy-start(f32[2,16,16,64]{3,2,1,0:T(8,128)} %get-tuple-element.190) | copy-start | bytes 393220
  205.5 12.2 %copy-start.9 = (f32[2,16,16,64]{3,2,1,0:T(8,128)S(1)}, f32[2,16,16,64]{3,2,1,0:T(8,128)}, u32[]{:S(2)}) copy-start(f32[2,16,16,64]{3,2,1,0:T(8,128)} %get-tuple-element.189) | copy-start | bytes 393220
  205.5 12.2 %copy-start.10 = (f32[2,16,16,64]{3,2,1,0:T(8,128)S(1)}, f32[2,16,16,64]{3,2,1,0:T(8,128)}, u32[]{:S(2)}) copy-start(f32[2,16,16,64]{3,2,1,0:T(8,128)} %get-tuple-element.191) | copy-start | bytes 393220
  205.5 12.2 %copy-start.28 = (pred[16,16]{1,0:T(8,128)(4,1)S(1)}, pred[16,16]{1,0:T(8,128)(4,1)}, u32[]{:S(2)}) copy-start(pred[16,16]{1,0:T(8,128)(4,1)} %iota_compare_fusion.1) | copy-start | bytes 772
  205.5 29.9 %all-to-all-start.2 = ((f32[2,64,1024]{2,0,1:T(2,128)}), f32[2,64,1024]{2,0,1:T(2,128)S(1)}, u32[]{:S(2)}, u32[]{:S(2)}) async-start(f32[2,64,1024]{2,0,1:T(2,128)} %reshape.497), calls=%async_computation.2 | async-start | bytes 1048576 | tf_op jit(solution)/shard_map/all_to_all | solution.py:222
  216.4 2.5 %copy-start.4 = (f32[6,64,16,64]{3,1,2,0:T(8,128)S(1)}, f32[6,64,16,64]{3,1,2,0:T(8,128)}, u32[]{:S(2)}) copy-start(f32[6,64,16,64]{3,1,2,0:T(8,128)} %get-tuple-element.79) | copy-start | bytes 4718596
  235.8 2.4 copy-start.1
  (11 other events, 16.1 us)
Sparse Core Ops, SparseCore 0:
  36.2 38.7 all-gather.4
  76.7 44.5 all-gather.2
where the time goes:
time: 246 us; the launch traced here: 245 us
  waiting for transfers between devices  54.8 us (22%)
  local copies, waits for them, and re-layouts  52.2 us (21%)
  matrix products  46.3 us (19%)
  other arithmetic  43.6 us (18%)
  starting transfers between devices  33.1 us (13%)
  between operations  14.8 us (6%)
    all_gather x1, waiting for transfers between devices, project(): lax.all_gather(decay_mixed_input, 'tp', axis=1, tiled=True)  33.6 us
    mul x6, other arithmetic, one_block(): keys_scaled = address_vectors_all * jnp.exp(middle - inclusive)  15 us
    all_to_all x1, starting transfers between devices, local(): lax.all_to_all(ordered_shift, 'rep', split_axis=0, concat_axis=1, tiled=T...  13 us
    dot_general x7, matrix products, one_block(): jnp.einsum('thi,hij->thj', accept_vectors_all * jnp.exp(exclusive), threa...  11.9 us
    all_to_all x1, starting transfers between devices, local(): lax.all_to_all(ret_state, 'rep', split_axis=1, concat_axis=0, tiled=True)  10.8 us
    dot_general x7, matrix products, one_block(): jnp.einsum('thi,shi->hts', recept_scaled, keys_scaled, precision=HIGH)  8.27 us
    dot_general x1, matrix products, project(): jnp.dot(lax.all_gather(mixed_value, 'tp', axis=1, tiled=True), content_ma...  8.09 us
    another operation x7, other arithmetic, one_block(): inclusive = jnp.cumsum(rate_b, axis=0)  8.08 us
  transfers between devices with their start and end apart: 6, of which 4 were waited for; matrix products, arithmetic and copies ran while one was open for 20% of the time, Pallas kernels for 0%

commit v1 on v0

--- a/solution.py
+++ b/solution.py
@@ -35,7 +35,15 @@
         preferred_element_type=jnp.float32,
     )
     decay_accumulated = jnp.dot(
-        lax.all_gather(decay_mixed_input, "tp", axis=1, tiled=True),
+        jnp.concatenate(
+            lax.all_to_all(
+                jnp.stack([decay_mixed_input] * lax.axis_size("tp"), axis=0),
+                split_axis=0,
+                axis_name="tp",
+                concat_axis=0,
+            ),
+            1,
+        ),
         forget_shrink_map,
         preferred_element_type=jnp.float32,
     )

time: 246 us -> 284 us (1.15)
  waiting for transfers between devices: 54.8 us -> 72 us
  starting transfers between devices: 33.1 us -> 43.9 us
  local copies, waits for them, and re-layouts: 52.2 us -> 62.1 us
    all_to_all x0 -> x1, waiting for transfers between devices: none -> 47.4 us  [project(): lax.all_to_all(jnp.stack([decay_mixed_input] * lax.axis_size('tp'), axis=...]
    all_gather x1 -> x0, waiting for transfers between devices: 33.6 us -> none  [project(): lax.all_gather(decay_mixed_input, 'tp', axis=1, tiled=True)]
    all_to_all x1, waiting for transfers between devices: 6.69 us -> 16.6 us  [local(): lax.all_to_all(ordered_state, 'rep', split_axis=0, concat_axis=1, tiled=T...]
    all_to_all x1, waiting for transfers between devices: 7.31 us -> 0.56 us  [local(): lax.all_to_all(ordered_shift, 'rep', split_axis=0, concat_axis=1, tiled=T...]
    all_to_all x1, starting transfers between devices: 4.42 us -> 9.74 us  [local(): lax.all_to_all(ret_shift, 'rep', split_axis=1, concat_axis=0, tiled=True)]
    all_to_all x0 -> x1, starting transfers between devices: none -> 4.84 us  [project(): lax.all_to_all(jnp.stack([decay_mixed_input] * lax.axis_size('tp'), axis=...]
    reshape x0 -> x1, local copies, waits for them, and re-layouts: none -> 4.29 us  [project(): jnp.concatenate(lax.all_to_all(jnp.stack([decay_mixed_input] * lax.axis_s...]
    unnamed x66 -> x60, local copies, waits for them, and re-layouts: 5.77 us -> 6.57 us
  transfers between devices with their start and end apart: 6 -> 6, of which waited for: 4 -> 4; matrix products, arithmetic and copies ran while one was open for 20% -> 22% of each run, Pallas kernels for 0% -> 0%
where the time goes in v1:
time: 284 us; the launch traced here: 283 us
  waiting for transfers between devices  72 us (25%)
  local copies, waits for them, and re-layouts  62.1 us (22%)
  matrix products  47.1 us (17%)
  starting transfers between devices  43.9 us (15%)
  other arithmetic  42.8 us (15%)
  between operations  14.7 us (5%)
    all_to_all x1, waiting for transfers between devices, project(): lax.all_to_all(jnp.stack([decay_mixed_input] * lax.axis_size('tp'), axis=...  47.4 us
    all_to_all x1, waiting for transfers between devices, local(): lax.all_to_all(ordered_state, 'rep', split_axis=0, concat_axis=1, tiled=T...  16.6 us
    mul x6, other arithmetic, one_block(): keys_scaled = address_vectors_all * jnp.exp(middle - inclusive)  15 us
    all_to_all x1, starting transfers between devices, local(): lax.all_to_all(ordered_shift, 'rep', split_axis=0, concat_axis=1, tiled=T...  13 us
    dot_general x7, matrix products, one_block(): jnp.einsum('thi,hij->thj', accept_vectors_all * jnp.exp(exclusive), threa...  11.9 us
    all_to_all x1, starting transfers between devices, local(): lax.all_to_all(ret_state, 'rep', split_axis=1, concat_axis=0, tiled=True)  10.8 us
    all_to_all x1, starting transfers between devices, local(): lax.all_to_all(ret_shift, 'rep', split_axis=1, concat_axis=0, tiled=True)  9.74 us
    dot_general x7, matrix products, one_block(): jnp.einsum('thi,shi->hts', recept_scaled, keys_scaled, precision=HIGH)  8.99 us
  transfers between devices with their start and end apart: 6, of which 4 were waited for; matrix products, arithmetic and copies ran while one was open for 22% of the time, Pallas kernels for 0%

profile of v1, /device:TPU:1, one launch (start us, length us, event | category | flops | bytes accessed | tf_op | source)
XLA Modules:
  0.0 282.9 jit_solution(13091516846290941439)
XLA Ops:
  10.2 13.0 %all-to-all-start.1 = ((bf16[128,1,16]{2,1,0:T(2,128)(2,1)}), bf16[128,1,16]{2,1,0:T(2,128)(2,1)S(1)}, u32[]{:S(2)}, u32[]{:S(2)}) async-start(bf16[128,1,16]{2,1,0:T(2,128)(2,1)} %convert.36), calls=%async_computation.1 | async-start | bytes 131072 | tf_op jit(solution)/shard_map/all_to_all | solution.py:151
  30.4 2.4 copy.157
  34.4 9.7 %all-to-all-start.4 = ((bf16[2,64,16]{2,0,1:T(2,128)(2,1)}), bf16[2,64,16]{2,0,1:T(2,128)(2,1)S(1)}, u32[]{:S(2)}, u32[]{:S(2)}) async-start(bf16[2,64,16]{2,0,1:T(2,128)(2,1)} %convert_bitcast_fusion), calls=%async_computation.4 | async-start | bytes 65536 | tf_op jit(solution)/shard_map/all_to_all | solution.py:231
  45.9 7.5 %all-to-all-done.4 = bf16[2,64,16]{2,0,1:T(2,128)(2,1)S(1)} async-done(((bf16[2,64,16]{2,0,1:T(2,128)(2,1)}), bf16[2,64,16]{2,0,1:T(2,128)(2,1)S(1)}, u32[]{:S(2)}, u32[]{:S(2)}) %all-to-all-start.4) | async-done | bytes 4128 | tf_op jit(solution)/shard_map/all_to_all | solution.py:231
  53.4 5.5 %all-to-all-start = ((f32[128,1,1024]{2,1,0:T(1,128)}), f32[128,1,1024]{2,1,0:T(1,128)}, u32[]{:S(2)}, u32[]{:S(2)}) async-start(f32[128,1,1024]{2,1,0:T(1,128)} %copy.157), calls=%async_computation | async-start | bytes 1048576 | tf_op jit(solution)/shard_map/all_to_all | solution.py:150
  60.1 16.6 %all-to-all-done = f32[128,1,1024]{2,1,0:T(1,128)} async-done(((f32[128,1,1024]{2,1,0:T(1,128)}), f32[128,1,1024]{2,1,0:T(1,128)}, u32[]{:S(2)}, u32[]{:S(2)}) %all-to-all-start) | async-done | bytes 524320 | tf_op jit(solution)/shard_map/all_to_all | solution.py:150
  76.7 2.2 stack.2
  78.9 4.8 %all-to-all-start.2 = ((bf16[4,416,1024]{2,1,0:T(8,128)(2,1)}), bf16[4,416,1024]{2,1,0:T(8,128)(2,1)}, u32[]{:S(2)}, u32[]{:S(2)}) async-start(bf16[4,416,1024]{2,1,0:T(8,128)(2,1)} %stack.2), calls=%async_computation.2 | async-start | bytes 6815744 | tf_op jit(solution)/shard_map/all_to_all | solution.py:39
  86.7 2.1 reshape.412
  88.8 2.2 reshape.410
  96.3 47.4 %all-to-all-done.2 = bf16[4,416,1024]{2,1,0:T(8,128)(2,1)} async-done(((bf16[4,416,1024]{2,1,0:T(8,128)(2,1)}), bf16[4,416,1024]{2,1,0:T(8,128)(2,1)}, u32[]{:S(2)}, u32[]{:S(2)}) %all-to-all-start.2) | async-done | bytes 3407904 | tf_op jit(solution)/shard_map/all_to_all | solution.py:39
  143.7 4.3 %copy.205 = bf16[4,52,8,1024]{3,2,0,1:T(8,128)(2,1)} copy(bf16[4,52,8,1024]{3,2,1,0:T(8,128)(2,1)} %bitcast.58) | data formatting | bytes 6815744 | tf_op jit(solution)/shard_map/reshape | solution.py:38
  147.9 3.7 %exponential_negate_fusion = f32[416,1024]{1,0:T(8,128)S(1)} fusion(bf16[128,1024]{1,0:T(8,128)(2,1)S(1)} %copy-done.15, bf16[416,4096]{1,0:T(8,128)(2,1)} %bitcast.184, bf16[4096,128]{1,0:T(8,128)(2,1)S(1)} %copy-done, f32[1024]{0:T(1024)} %param.31), kind=kOutput, calls=%fused_computation.44 | convolution fusion | flops 546164736 | bytes 6426624 | tf_op jit(solution)/shard_map/dot_general | solution.py:55
  154.5 1.9 select_multiply_fusion
  157.1 2.1 reshape_reshape.7
  161.2 8.1 %convolution_convert_fusion = bf16[416,1024]{1,0:T(8,128)(2,1)S(1)} fusion(bf16[416,4096]{1,0:T(8,128)(2,1)} %all-gather.2.cloned.1.call-done, bf16[4096,1024]{1,0:T(8,128)(2,1)} %param.28), kind=kOutput, calls=%fused_computation.48 | convolution fusion | flops 3490086912 | bytes 12648448 | tf_op jit(solution)/shard_map/dot_general | solution.py:32
  169.6 2.1 reshape.411
  171.7 60.3 %while.3 = (s32[]{:T(128)}, f32[16,64,64]{2,1,0:T(8,128)S(1)}, f32[6,64,16,64]{3,1,2,0:T(8,128)}, f32[6,64,16,64]{3,2,1,0:T(8,128)}, f32[6,64,16,64]{3,2,1,0:T(8...) while((s32[]{:T(128)}, f32[16,64,64]{2,1,0:T(8,128)S(1)}, ...), condition=%wide.region_3.4_spmd.clone, body=%wide.region_0.3_spmd.clone.sunk | while | flops 206572544 | bytes 8724625 | solution.py:100
  174.0 2.5 bitcast_multiply_fusion.6
  184.1 2.5 bitcast_multiply_fusion.6
  194.1 2.5 bitcast_multiply_fusion.6
  204.2 2.5 bitcast_multiply_fusion.6
  208.8 1.8 fusion.70
  214.2 2.5 bitcast_multiply_fusion.6
  224.3 2.5 bitcast_multiply_fusion.6
  228.9 1.8 fusion.70
  232.0 2.8 reduce_sum.64
  234.8 3.3 %multiply_reduce_fusion = f32[6,64,16]{1,2,0:T(8,128)S(1)} fusion(f32[6,64,16,64]{3,1,2,0:T(8,128)} %get-tuple-element.79, f32[6,64,16]{1,2,0:T(8,128)S(1)} %broadcast_multiply_fusion), kind=kLoop, calls=%fused_computation.40 | loop fusion | flops 1173504 | bytes 1622016 | tf_op jit(solution)/shard_map/reduce_sum | solution.py:14
  242.2 10.8 %all-to-all-start.3 = ((f32[2,64,1024]{2,0,1:T(2,128)}), f32[2,64,1024]{2,0,1:T(2,128)S(1)}, u32[]{:S(2)}, u32[]{:S(2)}) async-start(f32[2,64,1024]{2,0,1:T(2,128)} %reshape.507), calls=%async_computation.3 | async-start | bytes 1048576 | tf_op jit(solution)/shard_map/all_to_all | solution.py:230
  254.8 5.3 %copy.167 = f32[6,64,16,64]{3,2,1,0:T(8,128)} copy(f32[6,64,16,64]{3,1,2,0:T(8,128)} %get-tuple-element.79) | data formatting | bytes 3145728 | tf_op jit(solution)/shard_map/while | solution.py:100
  260.2 3.7 %reshape.407 = f32[1,384,1024]{2,1,0:T(8,128)} reshape(f32[6,64,16,64]{3,2,1,0:T(8,128)} %copy.167) | data formatting | bytes 3145728 | tf_op jit(solution)/shard_map/reshape | solution.py:111
  269.4 3.9 %fusion.26 = bf16[1,384,1024]{2,1,0:T(8,128)(2,1)} fusion(f32[1024]{0:T(1024)S(1)} %copy-done.23, f32[1024]{0:T(1024)S(1)} %copy-done.24, f32[1,384,1024]{2,1,0:T(8,128)} %copy.171, f32[1,384,1024]{2,1,0:T(8,128)} %reshape.407, f32[1,384,1024]{2,1,0:T(8,128)} %copy.169, pred[]{:T(512)S(1)} %bitcast.204), kind=kLoop, calls=%fused_computation.66 | loop fusion | flops 2359296 | bytes 5513217 | tf_op jit(solution)/shard_map/jit(_where)/select_n | solution.py:193
  (233 shorter events, 83.9 us)
Async XLA Ops:
  7.2 140.8 %copy-start = (bf16[4096,128]{1,0:T(8,128)(2,1)S(1)}, bf16[4096,128]{1,0:T(8,128)(2,1)}, u32[]{:S(2)}) copy-start(bf16[4096,128]{1,0:T(8,128)(2,1)} %param.29) | copy-start | bytes 3145732
  7.2 18.7 %copy-start.2 = (s32[128]{0:T(128)S(1)}, s32[128]{0:T(128)}, u32[]{:S(2)}) copy-start(s32[128]{0:T(128)} %param.40) | copy-start | bytes 1540
  7.2 19.3 %copy-start.7 = (bf16[1,384,1024]{2,1,0:T(8,128)(2,1)S(1)}, bf16[1,384,1024]{2,1,0:T(8,128)(2,1)}, u32[]{:S(2)}) copy-start(bf16[1,384,1024]{2,1,0:T(8,128)(2,1)} %param.22) | copy-start | bytes 2359300
  9.5 17.1 %copy-start.14 = (bf16[2,16,1024]{2,1,0:T(8,128)(2,1)S(1)}, bf16[2,16,1024]{2,1,0:T(8,128)(2,1)}, u32[]{:S(2)}) copy-start(bf16[2,16,1024]{2,1,0:T(8,128)(2,1)} %param.25) | copy-start | bytes 196612
  10.2 23.1 %all-to-all-start.1 = ((bf16[128,1,16]{2,1,0:T(2,128)(2,1)}), bf16[128,1,16]{2,1,0:T(2,128)(2,1)S(1)}, u32[]{:S(2)}, u32[]{:S(2)}) async-start(bf16[128,1,16]{2,1,0:T(2,128)(2,1)} %convert.36), calls=%async_computation.1 | async-start | bytes 131072 | tf_op jit(solution)/shard_map/all_to_all | solution.py:151
  28.8 15.4 %copy-start.21 = (f32[1024]{0:T(1024)S(1)}, f32[1024]{0:T(1024)}, u32[]{:S(2)}) copy-start(f32[1024]{0:T(1024)} %param.33) | copy-start | bytes 12292
  28.8 15.4 %copy-start.22 = (f32[1024]{0:T(1024)S(1)}, f32[1024]{0:T(1024)}, u32[]{:S(2)}) copy-start(f32[1024]{0:T(1024)} %param.34) | copy-start | bytes 12292
  34.4 19.0 %all-to-all-start.4 = ((bf16[2,64,16]{2,0,1:T(2,128)(2,1)}), bf16[2,64,16]{2,0,1:T(2,128)(2,1)S(1)}, u32[]{:S(2)}, u32[]{:S(2)}) async-start(bf16[2,64,16]{2,0,1:T(2,128)(2,1)} %convert_bitcast_fusion), calls=%async_computation.4 | async-start | bytes 65536 | tf_op jit(solution)/shard_map/all_to_all | solution.py:231
  45.8 13.2 %copy-start.9 = (bf16[384,1024]{1,0:T(8,128)(2,1)S(1)}, bf16[384,1024]{1,0:T(8,128)(2,1)}, u32[]{:S(2)}) copy-start(bf16[384,1024]{1,0:T(8,128)(2,1)} %get-tuple-element.184) | copy-start | bytes 2359300
  45.9 14.2 %copy-start.8 = (bf16[384,1024]{1,0:T(8,128)(2,1)S(1)}, bf16[384,1024]{1,0:T(8,128)(2,1)}, u32[]{:S(2)}) copy-start(bf16[384,1024]{1,0:T(8,128)(2,1)} %get-tuple-element.185) | copy-start | bytes 2359300
  53.4 23.3 %all-to-all-start = ((f32[128,1,1024]{2,1,0:T(1,128)}), f32[128,1,1024]{2,1,0:T(1,128)}, u32[]{:S(2)}, u32[]{:S(2)}) async-start(f32[128,1,1024]{2,1,0:T(1,128)} %copy.157), calls=%async_computation | async-start | bytes 1048576 | tf_op jit(solution)/shard_map/all_to_all | solution.py:150
  59.0 102.2 %all-gather.2.cloned.1.call-start = ((), (), s32[]{:S(2)}) async-start(), calls=%async_computation.5 | async-start | bytes 4259840 | tf_op jit(solution)/shard_map/all_gather | solution.py:33
  78.9 6.0 %copy-start.16 = (f32[1024]{0:T(1024)S(1)}, f32[1024]{0:T(1024)}, u32[]{:S(2)}) copy-start(f32[1024]{0:T(1024)} %param.32) | copy-start | bytes 12292
  78.9 6.1 %copy-start.18 = (bf16[2,16,1024]{2,1,0:T(8,128)(2,1)S(1)}, bf16[2,16,1024]{2,1,0:T(8,128)(2,1)}, u32[]{:S(2)}) copy-start(bf16[2,16,1024]{2,1,0:T(8,128)(2,1)} %param.26) | copy-start | bytes 196612
  78.9 7.0 %copy-start.19 = (bf16[2,16,1024]{2,1,0:T(8,128)(2,1)S(1)}, bf16[2,16,1024]{2,1,0:T(8,128)(2,1)}, u32[]{:S(2)}) copy-start(bf16[2,16,1024]{2,1,0:T(8,128)(2,1)} %param.27) | copy-start | bytes 196612
  78.9 7.8 %copy-start.12 = (bf16[1,384,1024]{2,1,0:T(8,128)(2,1)S(1)}, bf16[1,384,1024]{2,1,0:T(8,128)(2,1)}, u32[]{:S(2)}) copy-start(bf16[1,384,1024]{2,1,0:T(8,128)(2,1)} %param.23) | copy-start | bytes 2359300
  78.9 64.7 %all-to-all-start.2 = ((bf16[4,416,1024]{2,1,0:T(8,128)(2,1)}), bf16[4,416,1024]{2,1,0:T(8,128)(2,1)}, u32[]{:S(2)}, u32[]{:S(2)}) async-start(bf16[4,416,1024]{2,1,0:T(8,128)(2,1)} %stack.2), calls=%async_computation.2 | async-start | bytes 6815744 | tf_op jit(solution)/shard_map/all_to_all | solution.py:39
  86.7 2.1 copy-start.13
  91.6 4.5 %copy-start.26 = (s32[1024]{0:T(1024)}, s32[1024]{0:T(1024)S(1)}, u32[]{:S(2)}) copy-start(s32[1024]{0:T(1024)S(1)} %pad_clamp_fusion) | copy-start | bytes 12292
  143.7 4.3 %copy-start.15 = (bf16[128,1024]{1,0:T(8,128)(2,1)S(1)}, bf16[128,1024]{1,0:T(8,128)(2,1)}, u32[]{:S(2)}) copy-start(bf16[128,1024]{1,0:T(8,128)(2,1)} %param.30) | copy-start | bytes 786436
  152.9 4.1 %slice-start = ((f32[416,1024]{1,0:T(8,128)}), f32[384,1024]{1,0:T(8,128)S(1)}, s32[]{:S(2)}) async-start(f32[416,1024]{1,0:T(8,128)} %copy-done.6), calls=%async_computation.6 | async-start | bytes 3145728 | tf_op jit(solution)/shard_map/slice | solution.py:188
  157.1 2.7 copy-start.25
  186.6 2.1 copy-start.3
  196.7 2.1 copy-start.3
  206.8 2.1 copy-start.3
  216.8 2.1 copy-start.3
  234.8 3.7 %copy-start.5 = (f32[2,64,16,64]{3,2,1,0:T(8,128)S(1)}, f32[2,64,16,64]{3,2,1,0:T(8,128)}, u32[]{:S(2)}) copy-start(f32[2,64,16,64]{3,2,1,0:T(8,128)} %copy-done.4) | copy-start | bytes 1572868
  240.9 12.2 %copy-start.10 = (f32[2,16,16,64]{3,2,1,0:T(8,128)S(1)}, f32[2,16,16,64]{3,2,1,0:T(8,128)}, u32[]{:S(2)}) copy-start(f32[2,16,16,64]{3,2,1,0:T(8,128)} %get-tuple-element.190) | copy-start | bytes 393220
  242.2 12.2 %copy-start.11 = (f32[2,16,16,16]{3,2,1,0:T(8,128)S(1)}, f32[2,16,16,16]{3,2,1,0:T(8,128)}, u32[]{:S(2)}) copy-start(f32[2,16,16,16]{3,2,1,0:T(8,128)} %convolution_select_fusion.1) | copy-start | bytes 98308
  242.2 12.2 %copy-start.20 = (f32[2,16,16]{1,2,0:T(8,128)S(1)}, f32[2,16,16]{1,2,0:T(8,128)}, u32[]{:S(2)}) copy-start(f32[2,16,16]{1,2,0:T(8,128)} %copy.178) | copy-start | bytes 6148
  242.2 31.0 %all-to-all-start.3 = ((f32[2,64,1024]{2,0,1:T(2,128)}), f32[2,64,1024]{2,0,1:T(2,128)S(1)}, u32[]{:S(2)}, u32[]{:S(2)}) async-start(f32[2,64,1024]{2,0,1:T(2,128)} %reshape.507), calls=%async_computation.3 | async-start | bytes 1048576 | tf_op jit(solution)/shard_map/all_to_all | solution.py:230
  273.6 2.4 copy-start.1
  (8 other events, 11.6 us)
Sparse Core Ops, SparseCore 0:
  61.6 63.9 all-gather.1
